TPU v7x, 32 devices: a whole 2x2x4 slice. The times are simulated.
32 devices in a mesh: dp: 8 (over y, x, core), tensor: 4 (over z).
Axes of the slice: x: 2, y: 2, z: 4, core: 2. Of those that a mesh axis runs over, the one named last changes fastest.
Arguments:
- layer_input: bfloat16 [16, 768, 768], P('dp', 'tensor'), may hold values from -6 to 6
- word_segments: int32 [16, 256], P('dp'), may hold values from 0 to 13, never falling along the last dimension, each value on 1 to 36 neighbouring positions
- image_order: int32 [16, 14], P('dp'), may hold values from 0 to 13, each once within a row
- cross_qkv: bfloat16 [3, 768, 768], P(None, None, 'tensor'), may hold values from -0.21875 to 0.21875
- cross_out: bfloat16 [768, 768], P('tensor'), may hold values from -0.875 to 0.875
- self_qkv: bfloat16 [2, 3, 768, 768], P(None, None, None, 'tensor'), may hold values from -0.21875 to 0.21875
- self_out: bfloat16 [2, 768, 768], P(None, 'tensor'), may hold values from -0.875 to 0.875
- ffn_up: bfloat16 [2, 768, 3072], P(None, None, 'tensor'), may hold values from -0.21875 to 0.21875
- ffn_down: bfloat16 [2, 3072, 768], P(None, 'tensor'), may hold values from -0.109375 to 0.109375
- norm_gains: float32 [5, 768], replicated, may hold values from 0.5 to 1.5
- norm_biases: float32 [5, 768], replicated, may hold values from -3 to 3
- out_grad: bfloat16 [16, 768, 768], P('dp', 'tensor'), may hold values from -6 to 6
Outputs:
- layer_output: bfloat16 [16, 768, 768], P('dp', 'tensor')
- input_grad: float32 [16, 768, 768], P('dp', 'tensor')
- cross_qkv_grad: float32 [3, 768, 768], P(None, None, 'tensor')
- cross_out_grad: float32 [768, 768], P('tensor')
- self_qkv_grad: float32 [2, 3, 768, 768], P(None, None, None, 'tensor')
- self_out_grad: float32 [2, 768, 768], P(None, 'tensor')
- ffn_up_grad: float32 [2, 768, 3072], P(None, None, 'tensor')
- ffn_down_grad: float32 [2, 3072, 768], P(None, 'tensor')
- norm_gains_grad: float32 [5, 768], replicated
- norm_biases_grad: float32 [5, 768], replicated
Inputs may be any that keep to these rules, and one draw needn't show every extreme that they name: `word_segments`: in each row the ids never fall along the word slots, and each of the 14 captions has 1 to 36 slots. `image_order`: each row names every image once.
All inputs are finite; a program needn't handle non-finite values.
Results may differ from a plain program's by a relative error of at most 0.035.
Values may be sent and summed in bfloat16 or wider, within the bound.
A program may use at most 192 MiB of HBM per device.

v0:
```python
import jax
import jax.numpy as jnp
from jax import lax
from jax.sharding import PartitionSpec as P

HEAD_DIM = 64
WORDS = 256
CAPTIONS = 14
BOXES = 36
REGIONS = 504
PADS = 8
NORM_EPSILON = 1e-12


def contract_in(hidden, w_words, w_regions):
    if w_regions is None:
        return jnp.einsum("rsd,dc->rsc", hidden, w_words, preferred_element_type=jnp.float32)
    return jnp.concatenate(
        [
            jnp.einsum(
                "rsd,dc->rsc", hidden[:, :WORDS], w_words, preferred_element_type=jnp.float32
            ),
            jnp.einsum(
                "rsd,dc->rsc", hidden[:, WORDS:], w_regions, preferred_element_type=jnp.float32
            ),
        ],
        axis=1,
    )


def contract_back(grad_b, w_words, w_regions):
    if w_regions is None:
        return jnp.einsum("rsc,dc->rsd", grad_b, w_words, preferred_element_type=jnp.float32)
    return jnp.concatenate(
        [
            jnp.einsum(
                "rsc,dc->rsd", grad_b[:, :WORDS], w_words, preferred_element_type=jnp.float32
            ),
            jnp.einsum(
                "rsc,dc->rsd", grad_b[:, WORDS:], w_regions, preferred_element_type=jnp.float32
            ),
        ],
        axis=1,
    )


def weight_grad(hidden, grad_b, by_modality):
    if not by_modality:
        return jnp.einsum("rsd,rsc->dc", hidden, grad_b, preferred_element_type=jnp.float32)
    return jnp.stack(
        [
            jnp.einsum(
                "rsd,rsc->dc",
                hidden[:, :WORDS],
                grad_b[:, :WORDS],
                preferred_element_type=jnp.float32,
            ),
            jnp.einsum(
                "rsd,rsc->dc",
                hidden[:, WORDS:],
                grad_b[:, WORDS:],
                preferred_element_type=jnp.float32,
            ),
        ],
        axis=0,
    )


def head_split(tensor_b):
    return tensor_b.reshape(
        tensor_b.shape[0], tensor_b.shape[1], tensor_b.shape[2] // HEAD_DIM, HEAD_DIM
    )


def masked_scores(query_heads, key_heads, allowed):
    raw_scores = jnp.einsum(
        "rqhd,rkhd->rhqk", query_heads, key_heads, preferred_element_type=jnp.float32
    ) * HEAD_DIM ** (-0.5)
    return jnp.where(allowed[:, None], raw_scores, -1e30)


def region_matrix(table, member):
    if table is None:
        return None
    return table[member]


def attend(hidden, qkv_words, qkv_regions, out_words, out_regions, allowed):
    projected = [
        contract_in(hidden, qkv_words[member], region_matrix(qkv_regions, member)).astype(
            jnp.bfloat16
        )
        for member in range(3)
    ]
    query_b, key_b, value_b = projected
    scores = masked_scores(head_split(query_b), head_split(key_b), allowed)
    top_score = jnp.max(scores, axis=-1, keepdims=True)
    exponent = jnp.exp(scores - top_score)
    denominator = jnp.sum(exponent, axis=-1, keepdims=True)
    attention_probs = exponent / denominator
    log_total = top_score + jnp.log(denominator)
    context_b = (
        jnp.einsum(
            "rhqk,rkhd->rqhd",
            attention_probs.astype(jnp.bfloat16),
            head_split(value_b),
            preferred_element_type=jnp.float32,
        )
        .reshape(query_b.shape)
        .astype(jnp.bfloat16)
    )
    partial_out = contract_in(context_b, out_words, out_regions)
    return (partial_out, (query_b, key_b, value_b, log_total, context_b))


def attend_back(
    hidden, grad_b, kept_values, qkv_words, qkv_regions, out_words, out_regions, allowed
):
    query_b, key_b, value_b, log_total, context_b = kept_values
    by_modality = qkv_regions is not None
    out_weight_grad = weight_grad(context_b, grad_b, by_modality)
    context_grad = head_split(contract_back(grad_b, out_words, out_regions).astype(jnp.bfloat16))
    query_heads = head_split(query_b)
    key_heads = head_split(key_b)
    attention_probs = jnp.exp(masked_scores(query_heads, key_heads, allowed) - log_total)
    probs_grad = jnp.einsum(
        "rqhd,rkhd->rhqk", context_grad, head_split(value_b), preferred_element_type=jnp.float32
    )
    score_grad = (
        attention_probs
        * (probs_grad - jnp.sum(attention_probs * probs_grad, axis=-1, keepdims=True))
    ).astype(jnp.bfloat16)
    scaling = HEAD_DIM ** (-0.5)
    query_grad = (
        (
            jnp.einsum("rhqk,rkhd->rqhd", score_grad, key_heads, preferred_element_type=jnp.float32)
            * scaling
        )
        .reshape(query_b.shape)
        .astype(jnp.bfloat16)
    )
    key_grad = (
        (
            jnp.einsum(
                "rhqk,rqhd->rkhd", score_grad, query_heads, preferred_element_type=jnp.float32
            )
            * scaling
        )
        .reshape(key_b.shape)
        .astype(jnp.bfloat16)
    )
    value_grad = (
        jnp.einsum(
            "rhqk,rqhd->rkhd",
            attention_probs.astype(jnp.bfloat16),
            context_grad,
            preferred_element_type=jnp.float32,
        )
        .reshape(value_b.shape)
        .astype(jnp.bfloat16)
    )
    member_grads = [query_grad, key_grad, value_grad]
    qkv_grad = jnp.stack(
        [weight_grad(hidden, member_grads[member], by_modality) for member in range(3)],
        axis=1 if by_modality else 0,
    )
    hidden_grad = contract_back(query_grad, qkv_words[0], region_matrix(qkv_regions, 0))
    hidden_grad = hidden_grad + contract_back(key_grad, qkv_words[1], region_matrix(qkv_regions, 1))
    hidden_grad = hidden_grad + contract_back(
        value_grad, qkv_words[2], region_matrix(qkv_regions, 2)
    )
    return (hidden_grad, qkv_grad, out_weight_grad)


def norm_forward(summed, gain_rows, shift_rows):
    center = summed - jnp.mean(summed, axis=-1, keepdims=True)
    inverse = lax.rsqrt(jnp.mean(center * center, axis=-1, keepdims=True) + NORM_EPSILON)
    normed = center * inverse
    return (normed * gain_rows + shift_rows, normed, inverse)


def norm_backward(upstream, normed, inverse, gain_rows):
    scaled = upstream * gain_rows
    return inverse * (
        scaled
        - jnp.mean(scaled, axis=-1, keepdims=True)
        - normed * jnp.mean(scaled * normed, axis=-1, keepdims=True)
    )


def exact_gelu(values):
    return jax.nn.gelu(values, approximate=False)


def spread(piece_b):
    return lax.all_gather(piece_b, "tensor", axis=1, tiled=True)


def collect(partial_grad):
    return lax.psum_scatter(
        partial_grad.astype(jnp.bfloat16), "tensor", scatter_dimension=1, tiled=True
    ).astype(jnp.float32)


def widen(piece_b):
    return spread(piece_b)


def finish(partial_out):
    return lax.psum_scatter(
        partial_out.astype(jnp.bfloat16), "tensor", scatter_dimension=1, tiled=True
    ).astype(jnp.float32)


def back_sum(partial_grad):
    return collect(partial_grad)


def body(
    layer_input,
    word_segments,
    image_order,
    cross_qkv,
    cross_out,
    self_qkv,
    self_out,
    ffn_up,
    ffn_down,
    norm_gains,
    norm_biases,
    out_grad,
):
    row_count = layer_input.shape[0]
    share_len = layer_input.shape[1]
    slot_count = share_len * lax.axis_size("tensor")
    tensor_place = lax.axis_index("tensor")
    groups = jnp.concatenate(
        [
            word_segments,
            jnp.repeat(image_order, BOXES, axis=1),
            jnp.full((row_count, PADS), CAPTIONS, jnp.int32),
        ],
        axis=1,
    )
    slot_ids = jnp.arange(slot_count)
    slot_kind = jnp.where(slot_ids < WORDS, 0, jnp.where(slot_ids < WORDS + REGIONS, 1, 2))
    same_group = groups[:, :, None] == groups[:, None, :]
    differ = slot_kind[:, None] != slot_kind[None, :]
    cross_ok = same_group & (differ | (slot_kind[:, None] == 2))[None]
    self_ok = same_group & jnp.logical_not(differ)[None]
    stream_ids = tensor_place * share_len + jnp.arange(share_len)
    stream_word = (stream_ids < WORDS)[:, None]
    own_rows = (stream_ids // share_len == tensor_place).astype(jnp.float32)[:, None]
    word_weight = stream_word.astype(jnp.float32) * own_rows
    other_weight = own_rows - word_weight

    def pick(table, first_norm, second_norm):
        return jnp.where(stream_word, table[first_norm], table[second_norm])

    def norm_terms(upstream, normed, first_norm, second_norm, gain_grad, bias_grad):
        gain_terms = upstream * normed
        gain_grad = gain_grad.at[first_norm].add(jnp.sum(gain_terms * word_weight, axis=(0, 1)))
        gain_grad = gain_grad.at[second_norm].add(jnp.sum(gain_terms * other_weight, axis=(0, 1)))
        bias_grad = bias_grad.at[first_norm].add(jnp.sum(upstream * word_weight, axis=(0, 1)))
        bias_grad = bias_grad.at[second_norm].add(jnp.sum(upstream * other_weight, axis=(0, 1)))
        return (gain_grad, bias_grad)

    input_full = spread(layer_input)
    stream = layer_input.astype(jnp.float32)
    cross_part, cross_kept = attend(input_full, cross_qkv, None, cross_out, None, cross_ok)
    section_one, normed_one, inverse_one = norm_forward(
        stream + finish(cross_part), norm_gains[0], norm_biases[0]
    )
    one_full = widen(section_one.astype(jnp.bfloat16))
    self_part, self_kept = attend(
        one_full, self_qkv[0], self_qkv[1], self_out[0], self_out[1], self_ok
    )
    gains_two = pick(norm_gains, 1, 2)
    section_two, normed_two, inverse_two = norm_forward(
        section_one + finish(self_part), gains_two, pick(norm_biases, 1, 2)
    )
    two_full = widen(section_two.astype(jnp.bfloat16))
    upward = contract_in(two_full, ffn_up[0], ffn_up[1])
    active, gelu_pull = jax.vjp(exact_gelu, upward)
    active_b = active.astype(jnp.bfloat16)
    ffn_part = contract_in(active_b, ffn_down[0], ffn_down[1])
    gains_three = pick(norm_gains, 3, 4)
    result, normed_three, inverse_three = norm_forward(
        section_two + finish(ffn_part), gains_three, pick(norm_biases, 3, 4)
    )
    layer_output = result.astype(jnp.bfloat16)
    upstream = out_grad.astype(jnp.float32)
    gain_grad, bias_grad = norm_terms(
        upstream, normed_three, 3, 4, jnp.zeros_like(norm_gains), jnp.zeros_like(norm_biases)
    )
    grad_three = norm_backward(upstream, normed_three, inverse_three, gains_three)
    three_full = widen(grad_three.astype(jnp.bfloat16))
    down_grad = weight_grad(active_b, three_full, True)
    active_grad = contract_back(three_full, ffn_down[0], ffn_down[1])
    upward_grad = gelu_pull(active_grad)[0].astype(jnp.bfloat16)
    up_grad = weight_grad(two_full, upward_grad, True)
    section_two_grad = grad_three + back_sum(contract_back(upward_grad, ffn_up[0], ffn_up[1]))
    gain_grad, bias_grad = norm_terms(section_two_grad, normed_two, 1, 2, gain_grad, bias_grad)
    grad_two = norm_backward(section_two_grad, normed_two, inverse_two, gains_two)
    two_back = widen(grad_two.astype(jnp.bfloat16))
    hidden_two, self_qkv_grad, self_out_grad = attend_back(
        one_full, two_back, self_kept, self_qkv[0], self_qkv[1], self_out[0], self_out[1], self_ok
    )
    section_one_grad = grad_two + back_sum(hidden_two)
    gain_grad, bias_grad = norm_terms(section_one_grad, normed_one, 0, 0, gain_grad, bias_grad)
    grad_one = norm_backward(section_one_grad, normed_one, inverse_one, norm_gains[0])
    one_back = widen(grad_one.astype(jnp.bfloat16))
    hidden_one, cross_qkv_grad, cross_out_grad = attend_back(
        input_full, one_back, cross_kept, cross_qkv, None, cross_out, None, cross_ok
    )
    input_grad = grad_one + collect(hidden_one)
    summed_grads = [
        total.astype(jnp.float32)
        for total in lax.psum(
            [
                grad.astype(jnp.bfloat16)
                for grad in (
                    cross_qkv_grad,
                    cross_out_grad,
                    self_qkv_grad,
                    self_out_grad,
                    up_grad,
                    down_grad,
                )
            ],
            "dp",
        )
    ]
    norm_grads = lax.psum((gain_grad, bias_grad), ("dp", "tensor"))
    return (
        layer_output,
        input_grad,
        summed_grads[0],
        summed_grads[1],
        summed_grads[2],
        summed_grads[3],
        summed_grads[4],
        summed_grads[5],
        norm_grads[0],
        norm_grads[1],
    )


def solution(mesh):
    in_specs = (
        P("dp", "tensor", None),
        P("dp", None),
        P("dp", None),
        P(None, None, "tensor"),
        P("tensor", None),
        P(None, None, None, "tensor"),
        P(None, "tensor", None),
        P(None, None, "tensor"),
        P(None, "tensor", None),
        P(),
        P(),
        P("dp", "tensor", None),
    )
    out_specs = (
        P("dp", "tensor", None),
        P("dp", "tensor", None),
        P(None, None, "tensor"),
        P("tensor", None),
        P(None, None, None, "tensor"),
        P(None, "tensor", None),
        P(None, None, "tensor"),
        P(None, "tensor", None),
        P(),
        P(),
    )
    return jax.shard_map(body, mesh=mesh, in_specs=in_specs, out_specs=out_specs, check_vma=False)
```

profile of v0, /device:TPU:0, one launch (start us, length us, event | category | flops | bytes accessed | tf_op | source)
XLA Modules:
  0.0 923.2 jit_solution(17433531163479221925)
XLA Ops:
  10.3 2.4 compare_and_fusion.1
  12.7 50.1 %all-gather.7.cloned.1.call-done = bf16[2,768,768]{2,1,0:T(8,128)(2,1)} async-done(((bf16[2,192,768]{2,1,0:T(8,128)(2,1)}), bf16[2,768,768]{2,1,0:T(8,128)(2,1)}) %all-gather.7.cloned.1.call-update) | async-done | bytes 2359312 | tf_op jit(solution)/shard_map/all_gather | solution.py:196
  62.8 2.7 convolution_convert_fusion.8
  66.5 6.6 fusion.228
  73.1 6.9 fusion
  80.9 6.7 fusion.59
  88.5 2.2 convolution_convert_fusion
  91.5 46.3 %reduce-scatter.7.cloned.1.call-done = bf16[2,192,768]{2,1,0:T(8,128)(2,1)} async-done(((bf16[2,768,768]{2,1,0:T(8,128)(2,1)}), bf16[2,192,768]{2,1,0:T(8,128)(2,1)}) %reduce-scatter.7.cloned.1.call-update) | async-done | bytes 589840 | tf_op jit(solution)/shard_map/reduce_scatter | solution.py:210
  143.1 48.7 %all-gather.9.cloned.1.call-done = bf16[2,768,768]{2,1,0:T(8,128)(2,1)} async-done(((bf16[2,192,768]{2,1,0:T(8,128)(2,1)}), bf16[2,768,768]{2,1,0:T(8,128)(2,1)}) %all-gather.9.cloned.1.call-update) | async-done | bytes 2359312 | tf_op jit(solution)/shard_map/all_gather | solution.py:196
  191.8 1.8 convolution_convert_fusion.12
  193.6 1.7 convolution_convert_fusion.13
  196.8 6.5 fusion.229
  203.3 6.9 fusion.1
  211.3 6.6 fusion.58
  219.1 1.6 pad_maximum_fusion.2
  222.9 44.8 %reduce-scatter.9.cloned.1.call-done = bf16[2,192,768]{2,1,0:T(8,128)(2,1)} async-done(((bf16[2,768,768]{2,1,0:T(8,128)(2,1)}), bf16[2,192,768]{2,1,0:T(8,128)(2,1)}) %reduce-scatter.9.cloned.1.call-update) | async-done | bytes 589840 | tf_op jit(solution)/shard_map/reduce_scatter | solution.py:210
  267.7 1.7 fusion.225
  271.2 49.7 %all-gather.11.cloned.1.call-done = bf16[2,768,768]{2,1,0:T(8,128)(2,1)} async-done(((bf16[2,192,768]{2,1,0:T(8,128)(2,1)}), bf16[2,768,768]{2,1,0:T(8,128)(2,1)}) %all-gather.11.cloned.1.call-update) | async-done | bytes 2359312 | tf_op jit(solution)/shard_map/all_gather | solution.py:196
  320.9 2.4 fusion.102
  323.4 3.4 fusion.46
  326.8 11.2 %multiply_convert_fusion.2 = (bf16[2,768,768]{2,1,0:T(8,128)(2,1)S(1)}, f32[2,768,768]{2,1,0:T(8,128)}) fusion(f32[2,512,768]{2,1,0:T(8,128)S(1)} %fusion.46, f32[2,256,768]{2,1,0:T(8,128)S(1)} %fusion.102), kind=kLoop, calls=%fused_computation.33 | loop fusion | flops 77856768 | bytes 11796480 | tf_op jit(solution)/shard_map/convert_element_type | solution.py:285
  340.8 1.6 pad_maximum_fusion.3
  342.5 46.9 %reduce-scatter.11.cloned.1.call-done = bf16[2,192,768]{2,1,0:T(8,128)(2,1)} async-done(((bf16[2,768,768]{2,1,0:T(8,128)(2,1)}), bf16[2,192,768]{2,1,0:T(8,128)(2,1)}) %reduce-scatter.11.cloned.1.call-update) | async-done | bytes 589840 | tf_op jit(solution)/shard_map/reduce_scatter | solution.py:210
  389.4 1.9 fusion.223
  394.4 50.1 %all-gather.13.cloned.1.call-done = bf16[2,768,768]{2,1,0:T(8,128)(2,1)} async-done(((bf16[2,192,768]{2,1,0:T(8,128)(2,1)}), bf16[2,768,768]{2,1,0:T(8,128)(2,1)}) %all-gather.13.cloned.1.call-update) | async-done | bytes 2359312 | tf_op jit(solution)/shard_map/all_gather | solution.py:196
  444.5 2.5 fusion.96
  447.0 3.0 fusion.41
  450.0 3.8 add_convert_fusion.1
  456.1 1.6 pad_maximum_fusion.4
  457.9 46.8 %reduce-scatter.13.cloned.1.call-done = bf16[2,192,768]{2,1,0:T(8,128)(2,1)} async-done(((bf16[2,768,768]{2,1,0:T(8,128)(2,1)}), bf16[2,192,768]{2,1,0:T(8,128)(2,1)}) %reduce-scatter.13.cloned.1.call-update) | async-done | bytes 589840 | tf_op jit(solution)/shard_map/reduce_scatter | solution.py:200
  504.7 4.5 multiply_reduce_fusion.8
  511.5 1.9 fusion.227
  513.4 48.1 %all-gather.15.cloned.1.call-done = bf16[2,768,768]{2,1,0:T(8,128)(2,1)} async-done(((bf16[2,192,768]{2,1,0:T(8,128)(2,1)}), bf16[2,768,768]{2,1,0:T(8,128)(2,1)}) %all-gather.15.cloned.1.call-update) | async-done | bytes 2359312 | tf_op jit(solution)/shard_map/all_gather | solution.py:196
  561.6 1.6 convolution_convert_fusion.11
  563.2 2.3 fusion.72
  565.5 7.5 fusion.52
  573.0 1.6 fusion.170
  575.5 6.3 multiply_reduce_fusion.1
  581.8 6.9 multiply_convert_fusion.1
  588.7 2.2 fusion.49
  595.2 1.9 fusion.14
  597.9 46.3 %reduce-scatter.15.cloned.1.call-done = bf16[2,192,768]{2,1,0:T(8,128)(2,1)} async-done(((bf16[2,768,768]{2,1,0:T(8,128)(2,1)}), bf16[2,192,768]{2,1,0:T(8,128)(2,1)}) %reduce-scatter.15.cloned.1.call-update) | async-done | bytes 589840 | tf_op jit(solution)/shard_map/reduce_scatter | solution.py:200
  644.2 3.0 multiply_reduce_fusion.6
  649.6 3.3 fusion.34
  652.9 2.2 fusion.33
  655.1 1.6 pad_maximum_fusion.6
  660.9 1.6 pad_maximum_fusion.5
  671.1 28.6 %all-gather.17.cloned.1.call-done = bf16[2,768,768]{2,1,0:T(8,128)(2,1)} async-done(((bf16[2,192,768]{2,1,0:T(8,128)(2,1)}), bf16[2,768,768]{2,1,0:T(8,128)(2,1)}) %all-gather.17.cloned.1.call-update) | async-done | bytes 2359312 | tf_op jit(solution)/shard_map/all_gather | solution.py:196
  699.7 2.6 convolution_convert_fusion.7
  702.3 7.4 fusion.55
  709.8 10.3 %multiply_reduce_fusion = (f32[2,3,768]{2,1,0:T(4,128)S(1)}, f32[2,3,768,768]{2,3,1,0:T(8,128)}) fusion(f32[2,3,768,768]{2,3,1,0:T(8,128)} %get-tuple-element.240, f32[2,3,768]{2,1,0:T(4,128)S(1)} %log_add_fusion, bf16[2,768,3,64]{1,3,2,0:T(8,128)(2,1)S(1)} %bitcast.382, bf16[2,768,3,64]{1,3,2,0:T(8,128)(2,1)S(1)} %bitcast.390), kind=kOutput, calls=%fused_computation.1 | convolution fusion | flops 463597056 | bytes 29528064 | tf_op jit(solution)/shard_map/rqhd,rkhd->rhqk/dot_general | solution.py:126
  720.1 6.9 multiply_convert_fusion
  727.1 2.2 fusion.51
  735.9 1.9 fusion.185
  738.6 2.3 add_convert_fusion
  742.7 40.8 %all-reduce.2 = (f32[5,768]{1,0:T(8,128)}, f32[5,768]{1,0:T(8,128)}) all-reduce(f32[5,768]{1,0:T(8,128)S(1)} %scatter-add.49, f32[5,768]{1,0:T(8,128)S(1)} %scatter-add.59), channel_id=1, replica_groups=mesh['dp'=8,'tensor'=4] {'dp','tensor'}, use_global_device_ids=true, to_apply=%region_36.37 | all-reduce | flops 7680 | bytes 61440 | tf_op jit(solution)/shard_map/psum | solution.py:334
  783.5 79.2 %all-reduce.6.cloned.1.call-done = (bf16[2,3,768,192]{2,3,0,1:T(8,128)(2,1)}, bf16[3,768,192]{1,2,0:T(8,128)(2,1)}, bf16[192,768]{1,0:T(8,128)(2,1)}, bf16[2,192...) async-done(((bf16[2,3,768,192]{2,3,0,1:T(8,128)(2,1)}, bf16[3,768,192]{1,2,0:T(8,128)(2,1)}, bf16[192,768]{1,0:T(8,128)(2,1)}, ...) | async-done | bytes 8257552 | tf_op jit(solution)/shard_map/psum | solution.py:319
  862.8 1.9 convert_element_type.270
  864.7 2.2 convert_element_type.272
  866.9 2.1 copy.47
  871.3 2.5 convert_element_type.273
  874.1 2.5 convert_element_type.274
  876.7 36.9 %reduce-scatter.17.cloned.1.call-done = bf16[2,192,768]{2,1,0:T(8,128)(2,1)} async-done(((bf16[2,768,768]{2,1,0:T(8,128)(2,1)}), bf16[2,192,768]{2,1,0:T(8,128)(2,1)}) %reduce-scatter.17.cloned.1.call-update) | async-done | bytes 589840 | tf_op jit(solution)/shard_map/reduce_scatter | solution.py:200
  913.6 2.6 convert_add_fusion
  (342 shorter events, 62.2 us)
Async XLA Ops:
  7.2 81.3 %copy-start = (bf16[192,768]{1,0:T(8,128)(2,1)S(1)}, bf16[192,768]{1,0:T(8,128)(2,1)}, u32[]{:S(2)}) copy-start(bf16[192,768]{1,0:T(8,128)(2,1)} %param.40) | copy-start | bytes 884740
  7.2 55.6 %all-gather.7.cloned.1.call-start = ((), (), s32[]{:S(2)}) async-start(), calls=%async_computation.6 | async-start | bytes 2949120 | tf_op jit(solution)/shard_map/all_gather | solution.py:196
  7.9 129.9 %reduce-scatter.7.cloned.1.call-start = ((), (), s32[]{:S(2)}) async-start(), calls=%async_computation.7 | async-start | bytes 2949120 | tf_op jit(solution)/shard_map/reduce_scatter | solution.py:210
  9.6 53.2 %copy-start.38 = (bf16[3,768,192]{1,2,0:T(8,128)(2,1)S(1)}, bf16[3,768,192]{1,2,0:T(8,128)(2,1)}, u32[]{:S(2)}) copy-start(bf16[3,768,192]{1,2,0:T(8,128)(2,1)} %param.39) | copy-start | bytes 2654212
  65.6 7.5 copy-start.20
  66.5 6.6 copy-start.24
  73.1 7.9 copy-start.54
  80.0 7.7 copy-start.62
  80.9 6.8 copy-start.45
  88.5 49.3 %copy-start.1 = (bf16[2,192,768]{2,1,0:T(8,128)(2,1)S(1)}, bf16[2,192,768]{2,1,0:T(8,128)(2,1)}, u32[]{:S(2)}) copy-start(bf16[2,192,768]{2,1,0:T(8,128)(2,1)} %param.36) | copy-start | bytes 1769476
  90.8 101.1 %all-gather.9.cloned.1.call-start = ((), (), s32[]{:S(2)}) async-start(), calls=%async_computation.8 | async-start | bytes 2949120 | tf_op jit(solution)/shard_map/all_gather | solution.py:196
  91.5 50.5 %copy-start.13 = (bf16[2,3,768,192]{2,3,1,0:T(8,128)(2,1)S(1)}, bf16[2,3,768,192]{2,3,1,0:T(8,128)(2,1)}, u32[]{:S(2)}) copy-start(bf16[2,3,768,192]{2,3,1,0:T(8,128)(2,1)} %param.41) | copy-start | bytes 5308420
  137.8 2.8 copy-start.3
  141.7 126.0 %reduce-scatter.9.cloned.1.call-start = ((), (), s32[]{:S(2)}) async-start(), calls=%async_computation.9 | async-start | bytes 2949120 | tf_op jit(solution)/shard_map/reduce_scatter | solution.py:210
  143.1 52.2 %copy-start.53 = (bf16[1,1,768,192]{2,3,1,0:T(8,128)(2,1)S(1)}, bf16[1,1,768,192]{2,3,1,0:T(8,128)(2,1)}, u32[]{:S(2)}) copy-start(bf16[1,1,768,192]{2,3,1,0:T(8,128)(2,1)} %get-tuple-element.227) | copy-start | bytes 884740
  191.8 3.5 copy-start.94
  193.6 3.1 copy-start.58
  196.0 7.2 copy-start.49
  196.7 6.5 copy-start.47
  203.2 8.1 copy-start.64
  203.3 7.4 copy-start.51
  210.2 7.8 copy-start.66
  210.6 7.3 copy-start.56
  211.3 6.7 copy-start.28
  220.7 100.2 %all-gather.11.cloned.1.call-start = ((), (), s32[]{:S(2)}) async-start(), calls=%async_computation.10 | async-start | bytes 2949120 | tf_op jit(solution)/shard_map/all_gather | solution.py:196
  270.8 118.6 %reduce-scatter.11.cloned.1.call-start = ((), (), s32[]{:S(2)}) async-start(), calls=%async_computation.11 | async-start | bytes 2949120 | tf_op jit(solution)/shard_map/reduce_scatter | solution.py:210
  323.4 3.4 copy-start.16
  326.8 11.2 %copy-start.7 = (f32[2,512,768]{2,1,0:T(8,128)}, f32[2,512,768]{2,1,0:T(8,128)S(1)}, u32[]{:S(2)}) copy-start(f32[2,512,768]{2,1,0:T(8,128)S(1)} %fusion.46) | copy-start | bytes 9437188
  326.8 11.2 %copy-start.88 = (bf16[2,768,768]{2,1,0:T(8,128)(2,1)S(1)}, bf16[2,768,768]{2,1,0:T(8,128)(2,1)}, u32[]{:S(2)}) copy-start(bf16[2,768,768]{2,1,0:T(8,128)(2,1)} %param.44) | copy-start | bytes 7077892
  342.4 102.1 %all-gather.13.cloned.1.call-start = ((), (), s32[]{:S(2)}) async-start(), calls=%async_computation.12 | async-start | bytes 2949120 | tf_op jit(solution)/shard_map/all_gather | solution.py:196
  342.5 162.2 %copy-start.68 = (f32[192]{0:T(256)}, f32[192]{0:T(256)S(1)}, u32[]{:S(2)}) copy-start(f32[192]{0:T(256)S(1)} %get-tuple-element.248) | copy-start | bytes 2308
  394.4 110.3 %reduce-scatter.13.cloned.1.call-start = ((), (), s32[]{:S(2)}) async-start(), calls=%async_computation.13 | async-start | bytes 2949120 | tf_op jit(solution)/shard_map/reduce_scatter | solution.py:200
  447.0 3.0 copy-start.8
  447.0 3.0 copy-start.17
  450.0 3.8 copy-start.91
  457.7 103.9 %all-gather.15.cloned.1.call-start = ((), (), s32[]{:S(2)}) async-start(), calls=%async_computation.14 | async-start | bytes 2949120 | tf_op jit(solution)/shard_map/all_gather | solution.py:196
  504.7 5.5 copy-start.6
  510.2 3.2 copy-start.65
  510.2 3.2 copy-start.67
  510.2 64.9 %slice-start.4 = ((s8[14155776]{0:T(1024)(128)(4,1)}), s8[1572864]{0:T(1024)(128)(4,1)S(1)}, s32[]{:S(2)}) async-start(s8[14155776]{0:T(1024)(128)(4,1)} %bitcast.357), calls=%async_computation.23 | async-start | bytes 3145728
  511.4 132.8 %reduce-scatter.15.cloned.1.call-start = ((), (), s32[]{:S(2)}) async-start(), calls=%async_computation.15 | async-start | bytes 2949120 | tf_op jit(solution)/shard_map/reduce_scatter | solution.py:200
  563.2 12.0 %slice-start.5 = ((s8[14155776]{0:T(1024)(128)(4,1)}), s8[4194304]{0:T(1024)(128)(4,1)S(1)}, s32[]{:S(2)}) async-start(s8[14155776]{0:T(1024)(128)(4,1)} %bitcast.357), calls=%async_computation.24 | async-start | bytes 8388608
  565.4 7.5 copy-start.14
  565.5 9.7 %slice-start.6 = ((s8[14155776]{0:T(1024)(128)(4,1)}), s8[4194304]{0:T(1024)(128)(4,1)S(1)}, s32[]{:S(2)}) async-start(s8[14155776]{0:T(1024)(128)(4,1)} %bitcast.357), calls=%async_computation.25 | async-start | bytes 8388608
  565.5 9.7 %slice-start.7 = ((s8[14155776]{0:T(1024)(128)(4,1)}), s8[4194304]{0:T(1024)(128)(4,1)S(1)}, s32[]{:S(2)}) async-start(s8[14155776]{0:T(1024)(128)(4,1)} %bitcast.357), calls=%async_computation.26 | async-start | bytes 8388608
  581.8 6.9 copy-start.48
  581.8 6.9 copy-start.61
  591.0 2.8 copy-start.31
  597.2 47.0 %copy-start.2 = (bf16[2,192,768]{2,1,0:T(8,128)(2,1)S(1)}, bf16[2,192,768]{2,1,0:T(8,128)(2,1)}, u32[]{:S(2)}) copy-start(bf16[2,192,768]{2,1,0:T(8,128)(2,1)} %param.36) | copy-start | bytes 1769476
  597.2 47.0 %copy-start.4 = (bf16[2,192,768]{2,1,0:T(8,128)(2,1)S(1)}, bf16[2,192,768]{2,1,0:T(8,128)(2,1)}, u32[]{:S(2)}) copy-start(bf16[2,192,768]{2,1,0:T(8,128)(2,1)} %reduce-scatter.7.cloned.1.call-done) | copy-start | bytes 1769476
  597.2 47.0 %copy-start.69 = (f32[192]{0:T(256)S(1)}, f32[192]{0:T(256)}, u32[]{:S(2)}) copy-start(f32[192]{0:T(256)} %copy-done.68) | copy-start | bytes 2308
  597.2 102.5 %all-gather.17.cloned.1.call-start = ((), (), s32[]{:S(2)}) async-start(), calls=%async_computation.16 | async-start | bytes 2949120 | tf_op jit(solution)/shard_map/all_gather | solution.py:196
  649.5 213.2 %all-reduce.6.cloned.1.call-start = ((), (), s32[]{:S(2)}) async-start(), calls=%async_computation.18 | async-start | bytes 16515072 | tf_op jit(solution)/shard_map/psum | solution.py:319
  655.1 3.5 copy-start.96
  702.2 7.5 copy-start.46
  702.3 17.8 %slice-start = ((s8[14155776]{0:T(1024)(128)(4,1)}), s8[4194304]{0:T(1024)(128)(4,1)S(1)}, s32[]{:S(2)}) async-start(s8[14155776]{0:T(1024)(128)(4,1)} %bitcast.355), calls=%async_computation.19 | async-start | bytes 8388608
  702.3 17.8 %slice-start.1 = ((s8[14155776]{0:T(1024)(128)(4,1)}), s8[4194304]{0:T(1024)(128)(4,1)S(1)}, s32[]{:S(2)}) async-start(s8[14155776]{0:T(1024)(128)(4,1)} %bitcast.355), calls=%async_computation.20 | async-start | bytes 8388608
  709.7 10.3 %slice-start.2 = ((s8[14155776]{0:T(1024)(128)(4,1)}), s8[4194304]{0:T(1024)(128)(4,1)S(1)}, s32[]{:S(2)}) async-start(s8[14155776]{0:T(1024)(128)(4,1)} %bitcast.355), calls=%async_computation.21 | async-start | bytes 8388608
  709.7 10.3 %slice-start.3 = ((s8[14155776]{0:T(1024)(128)(4,1)}), s8[1572864]{0:T(1024)(128)(4,1)S(1)}, s32[]{:S(2)}) async-start(s8[14155776]{0:T(1024)(128)(4,1)} %bitcast.355), calls=%async_computation.22 | async-start | bytes 3145728
  720.1 7.0 copy-start.25
  735.8 177.8 %reduce-scatter.17.cloned.1.call-start = ((), (), s32[]{:S(2)}) async-start(), calls=%async_computation.17 | async-start | bytes 2949120 | tf_op jit(solution)/shard_map/reduce_scatter | solution.py:200
  862.7 4.1 copy-start.36
  871.3 2.9 copy-start.26
  874.1 39.5 %copy-start.10 = (f32[2,192,768]{2,1,0:T(8,128)S(1)}, f32[2,192,768]{2,1,0:T(8,128)}, u32[]{:S(2)}) copy-start(f32[2,192,768]{2,1,0:T(8,128)} %copy-done.9) | copy-start | bytes 3538948
  (56 other events, 84.4 us)
Sparse Core Ops, SparseCore 0:
  9.6 53.1 all-gather.6
  90.9 46.8 reduce-scatter.6
  141.8 49.9 all-gather.8
  220.8 46.8 reduce-scatter.8
  270.9 49.9 all-gather.10
  342.5 46.8 reduce-scatter.10
  394.5 49.9 all-gather.12
  457.8 46.8 reduce-scatter.12
  511.6 49.9 all-gather.14
  597.3 46.8 reduce-scatter.14
  649.6 49.9 all-gather.16
  735.9 126.7 all-reduce.5
  865.2 48.4 reduce-scatter.16
where the time goes:
time: 932 us; the launch traced here: 923 us
  waiting for transfers between devices  624 us (67%)
  matrix products  124 us (13%)
  other arithmetic  96.2 us (10%)
  blocking collectives  40.8 us (4%)
  local copies, waits for them, and re-layouts  20.7 us (2%)
  between operations  16 us (2%)
    all_gather x6, waiting for transfers between devices, spread(): return lax.all_gather(piece_b, 'tensor', axis=1, tiled=True)  275 us
    reduce_scatter x3, waiting for transfers between devices, finish(): lax.psum_scatter(partial_out.astype(jnp.bfloat16), 'tensor', scatter_dime...  138 us
    reduce_scatter x3, waiting for transfers between devices, collect(): lax.psum_scatter(partial_grad.astype(jnp.bfloat16), 'tensor', scatter_dim...  130 us
    psum x1, waiting for transfers between devices, body(): lax.psum([grad.astype(jnp.bfloat16) for grad in (cross_qkv_grad, cross_ou...  79.2 us
    psum x1, blocking collectives, body(): norm_grads = lax.psum((gain_grad, bias_grad), ('dp', 'tensor'))  40.8 us
  transfers between devices with their start and end apart: 13, of which 13 were waited for; matrix products, arithmetic and copies ran while one was open for 5% of the time, Pallas kernels for 0%

commit v1 on v0

--- a/solution.py
+++ b/solution.py
@@ -331,7 +331,7 @@
             "dp",
         )
     ]
-    norm_grads = lax.psum((gain_grad, bias_grad), ("dp", "tensor"))
+    norm_grads = lax.psum(lax.psum((gain_grad, bias_grad), "tensor"), "dp")
     return (
         layer_output,
         input_grad,

time: 932 us -> 932 us (level)
    psum x1 -> x2, blocking collectives: 40.8 us -> 41.7 us  [body(): norm_grads = lax.psum(lax.psum((gain_grad, bias_grad), 'tensor'), 'dp')]
where the time goes in v1:
time: 932 us; the launch traced here: 923 us
  waiting for transfers between devices  623 us (67%)
  matrix products  124 us (13%)
  other arithmetic  96.3 us (10%)
  blocking collectives  41.7 us (4%)
  local copies, waits for them, and re-layouts  20.7 us (2%)
  between operations  16 us (2%)
    all_gather x6, waiting for transfers between devices, spread(): return lax.all_gather(piece_b, 'tensor', axis=1, tiled=True)  275 us
    reduce_scatter x3, waiting for transfers between devices, finish(): lax.psum_scatter(partial_out.astype(jnp.bfloat16), 'tensor', scatter_dime...  138 us
    reduce_scatter x3, waiting for transfers between devices, collect(): lax.psum_scatter(partial_grad.astype(jnp.bfloat16), 'tensor', scatter_dim...  130 us
    psum x1, waiting for transfers between devices, body(): lax.psum([grad.astype(jnp.bfloat16) for grad in (cross_qkv_grad, cross_ou...  78.3 us
    psum x2, blocking collectives, body(): norm_grads = lax.psum(lax.psum((gain_grad, bias_grad), 'tensor'), 'dp')  41.7 us
  transfers between devices with their start and end apart: 13, of which 13 were waited for; matrix products, arithmetic and copies ran while one was open for 5% of the time, Pallas kernels for 0%

profile of v1, /device:TPU:0, one launch (start us, length us, event | category | flops | bytes accessed | tf_op | source)
XLA Modules:
  0.0 923.2 jit_solution(14335918508543927066)
XLA Ops:
  10.3 2.4 compare_and_fusion.1
  12.7 50.1 %all-gather.7.cloned.1.call-done = bf16[2,768,768]{2,1,0:T(8,128)(2,1)} async-done(((bf16[2,192,768]{2,1,0:T(8,128)(2,1)}), bf16[2,768,768]{2,1,0:T(8,128)(2,1)}) %all-gather.7.cloned.1.call-update) | async-done | bytes 2359312 | tf_op jit(solution)/shard_map/all_gather | solution.py:196
  62.8 2.7 convolution_convert_fusion.8
  66.5 6.6 fusion.228
  73.1 6.9 fusion
  80.9 6.7 fusion.59
  88.5 2.2 convolution_convert_fusion
  91.5 46.3 %reduce-scatter.7.cloned.1.call-done = bf16[2,192,768]{2,1,0:T(8,128)(2,1)} async-done(((bf16[2,768,768]{2,1,0:T(8,128)(2,1)}), bf16[2,192,768]{2,1,0:T(8,128)(2,1)}) %reduce-scatter.7.cloned.1.call-update) | async-done | bytes 589840 | tf_op jit(solution)/shard_map/reduce_scatter | solution.py:210
  143.1 48.7 %all-gather.9.cloned.1.call-done = bf16[2,768,768]{2,1,0:T(8,128)(2,1)} async-done(((bf16[2,192,768]{2,1,0:T(8,128)(2,1)}), bf16[2,768,768]{2,1,0:T(8,128)(2,1)}) %all-gather.9.cloned.1.call-update) | async-done | bytes 2359312 | tf_op jit(solution)/shard_map/all_gather | solution.py:196
  191.8 1.8 convolution_convert_fusion.12
  193.6 1.7 convolution_convert_fusion.13
  196.8 6.5 fusion.229
  203.3 6.9 fusion.1
  211.3 6.6 fusion.58
  219.1 1.6 pad_maximum_fusion.2
  222.9 44.8 %reduce-scatter.9.cloned.1.call-done = bf16[2,192,768]{2,1,0:T(8,128)(2,1)} async-done(((bf16[2,768,768]{2,1,0:T(8,128)(2,1)}), bf16[2,192,768]{2,1,0:T(8,128)(2,1)}) %reduce-scatter.9.cloned.1.call-update) | async-done | bytes 589840 | tf_op jit(solution)/shard_map/reduce_scatter | solution.py:210
  267.7 1.7 fusion.225
  271.2 49.7 %all-gather.11.cloned.1.call-done = bf16[2,768,768]{2,1,0:T(8,128)(2,1)} async-done(((bf16[2,192,768]{2,1,0:T(8,128)(2,1)}), bf16[2,768,768]{2,1,0:T(8,128)(2,1)}) %all-gather.11.cloned.1.call-update) | async-done | bytes 2359312 | tf_op jit(solution)/shard_map/all_gather | solution.py:196
  320.9 2.4 fusion.102
  323.4 3.4 fusion.46
  326.8 11.2 %multiply_convert_fusion.2 = (bf16[2,768,768]{2,1,0:T(8,128)(2,1)S(1)}, f32[2,768,768]{2,1,0:T(8,128)}) fusion(f32[2,512,768]{2,1,0:T(8,128)S(1)} %fusion.46, f32[2,256,768]{2,1,0:T(8,128)S(1)} %fusion.102), kind=kLoop, calls=%fused_computation.33 | loop fusion | flops 77856768 | bytes 11796480 | tf_op jit(solution)/shard_map/convert_element_type | solution.py:285
  340.8 1.6 pad_maximum_fusion.3
  342.5 46.9 %reduce-scatter.11.cloned.1.call-done = bf16[2,192,768]{2,1,0:T(8,128)(2,1)} async-done(((bf16[2,768,768]{2,1,0:T(8,128)(2,1)}), bf16[2,192,768]{2,1,0:T(8,128)(2,1)}) %reduce-scatter.11.cloned.1.call-update) | async-done | bytes 589840 | tf_op jit(solution)/shard_map/reduce_scatter | solution.py:210
  389.4 1.9 fusion.223
  394.4 50.1 %all-gather.13.cloned.1.call-done = bf16[2,768,768]{2,1,0:T(8,128)(2,1)} async-done(((bf16[2,192,768]{2,1,0:T(8,128)(2,1)}), bf16[2,768,768]{2,1,0:T(8,128)(2,1)}) %all-gather.13.cloned.1.call-update) | async-done | bytes 2359312 | tf_op jit(solution)/shard_map/all_gather | solution.py:196
  444.5 2.5 fusion.96
  447.0 3.0 fusion.41
  450.0 3.8 add_convert_fusion.1
  456.1 1.6 pad_maximum_fusion.4
  457.9 46.8 %reduce-scatter.13.cloned.1.call-done = bf16[2,192,768]{2,1,0:T(8,128)(2,1)} async-done(((bf16[2,768,768]{2,1,0:T(8,128)(2,1)}), bf16[2,192,768]{2,1,0:T(8,128)(2,1)}) %reduce-scatter.13.cloned.1.call-update) | async-done | bytes 589840 | tf_op jit(solution)/shard_map/reduce_scatter | solution.py:200
  504.7 4.5 multiply_reduce_fusion.8
  511.5 1.9 fusion.227
  513.4 48.1 %all-gather.15.cloned.1.call-done = bf16[2,768,768]{2,1,0:T(8,128)(2,1)} async-done(((bf16[2,192,768]{2,1,0:T(8,128)(2,1)}), bf16[2,768,768]{2,1,0:T(8,128)(2,1)}) %all-gather.15.cloned.1.call-update) | async-done | bytes 2359312 | tf_op jit(solution)/shard_map/all_gather | solution.py:196
  561.6 1.6 convolution_convert_fusion.11
  563.2 2.3 fusion.72
  565.5 7.5 fusion.52
  575.5 6.3 multiply_reduce_fusion.1
  581.8 6.9 multiply_convert_fusion.1
  588.8 2.2 fusion.49
  595.3 1.9 fusion.14
  598.0 46.3 %reduce-scatter.15.cloned.1.call-done = bf16[2,192,768]{2,1,0:T(8,128)(2,1)} async-done(((bf16[2,768,768]{2,1,0:T(8,128)(2,1)}), bf16[2,192,768]{2,1,0:T(8,128)(2,1)}) %reduce-scatter.15.cloned.1.call-update) | async-done | bytes 589840 | tf_op jit(solution)/shard_map/reduce_scatter | solution.py:200
  644.2 3.0 multiply_reduce_fusion.6
  649.6 3.3 fusion.34
  652.9 2.2 fusion.33
  655.1 1.6 pad_maximum_fusion.6
  660.9 1.6 pad_maximum_fusion.5
  671.1 28.6 %all-gather.17.cloned.1.call-done = bf16[2,768,768]{2,1,0:T(8,128)(2,1)} async-done(((bf16[2,192,768]{2,1,0:T(8,128)(2,1)}), bf16[2,768,768]{2,1,0:T(8,128)(2,1)}) %all-gather.17.cloned.1.call-update) | async-done | bytes 2359312 | tf_op jit(solution)/shard_map/all_gather | solution.py:196
  699.7 2.6 convolution_convert_fusion.7
  702.3 7.4 fusion.55
  709.8 10.3 %multiply_reduce_fusion = (f32[2,3,768]{2,1,0:T(4,128)S(1)}, f32[2,3,768,768]{2,3,1,0:T(8,128)}) fusion(f32[2,3,768,768]{2,3,1,0:T(8,128)} %get-tuple-element.242, f32[2,3,768]{2,1,0:T(4,128)S(1)} %log_add_fusion, bf16[2,768,3,64]{1,3,2,0:T(8,128)(2,1)S(1)} %bitcast.382, bf16[2,768,3,64]{1,3,2,0:T(8,128)(2,1)S(1)} %bitcast.390), kind=kOutput, calls=%fused_computation.1 | convolution fusion | flops 463597056 | bytes 29528064 | tf_op jit(solution)/shard_map/rqhd,rkhd->rhqk/dot_general | solution.py:126
  720.1 6.9 multiply_convert_fusion
  727.1 2.2 fusion.51
  735.9 1.9 fusion.185
  738.6 2.3 add_convert_fusion
  742.7 16.9 %all-reduce.3 = (f32[5,768]{1,0:T(8,128)S(1)}, f32[5,768]{1,0:T(8,128)S(1)}) all-reduce(f32[5,768]{1,0:T(8,128)S(1)} %scatter-add.49, f32[5,768]{1,0:T(8,128)S(1)} %scatter-add.59), channel_id=1, replica_groups=mesh['dp'=8,'tensor'=4] {'tensor'}, use_global_device_ids=true, to_apply=%region_36.37 | all-reduce | flops 7680 | bytes 61440 | tf_op jit(solution)/shard_map/psum | solution.py:334
  759.7 24.8 %all-reduce.2 = (f32[5,768]{1,0:T(8,128)}, f32[5,768]{1,0:T(8,128)}) all-reduce(f32[5,768]{1,0:T(8,128)S(1)} %get-tuple-element.204, f32[5,768]{1,0:T(8,128)S(1)} %get-tuple-element.205), channel_id=1, replica_groups=mesh['dp'=8,'tensor'=4] {'dp'}, use_global_device_ids=true, to_apply=%region_37.38 | all-reduce | flops 7680 | bytes 61440 | tf_op jit(solution)/shard_map/psum | solution.py:334
  784.5 78.3 %all-reduce.7.cloned.1.call-done = (bf16[2,3,768,192]{2,3,0,1:T(8,128)(2,1)}, bf16[3,768,192]{1,2,0:T(8,128)(2,1)}, bf16[192,768]{1,0:T(8,128)(2,1)}, bf16[2,192...) async-done(((bf16[2,3,768,192]{2,3,0,1:T(8,128)(2,1)}, bf16[3,768,192]{1,2,0:T(8,128)(2,1)}, bf16[192,768]{1,0:T(8,128)(2,1)}, ...) | async-done | bytes 8257552 | tf_op jit(solution)/shard_map/psum | solution.py:319
  862.7 1.9 convert_element_type.270
  864.7 2.2 convert_element_type.272
  866.8 2.1 copy.47
  871.3 2.5 convert_element_type.273
  874.1 2.5 convert_element_type.274
  876.7 36.9 %reduce-scatter.17.cloned.1.call-done = bf16[2,192,768]{2,1,0:T(8,128)(2,1)} async-done(((bf16[2,768,768]{2,1,0:T(8,128)(2,1)}), bf16[2,192,768]{2,1,0:T(8,128)(2,1)}) %reduce-scatter.17.cloned.1.call-update) | async-done | bytes 589840 | tf_op jit(solution)/shard_map/reduce_scatter | solution.py:200
  913.6 2.6 convert_add_fusion
  (343 shorter events, 63.8 us)
Async XLA Ops:
  7.2 81.3 %copy-start = (bf16[192,768]{1,0:T(8,128)(2,1)S(1)}, bf16[192,768]{1,0:T(8,128)(2,1)}, u32[]{:S(2)}) copy-start(bf16[192,768]{1,0:T(8,128)(2,1)} %param.40) | copy-start | bytes 884740
  7.2 55.6 %all-gather.7.cloned.1.call-start = ((), (), s32[]{:S(2)}) async-start(), calls=%async_computation.6 | async-start | bytes 2949120 | tf_op jit(solution)/shard_map/all_gather | solution.py:196
  7.9 129.9 %reduce-scatter.7.cloned.1.call-start = ((), (), s32[]{:S(2)}) async-start(), calls=%async_computation.7 | async-start | bytes 2949120 | tf_op jit(solution)/shard_map/reduce_scatter | solution.py:210
  9.6 53.2 %copy-start.38 = (bf16[3,768,192]{1,2,0:T(8,128)(2,1)S(1)}, bf16[3,768,192]{1,2,0:T(8,128)(2,1)}, u32[]{:S(2)}) copy-start(bf16[3,768,192]{1,2,0:T(8,128)(2,1)} %param.39) | copy-start | bytes 2654212
  65.6 7.5 copy-start.20
  66.5 6.6 copy-start.24
  73.1 7.9 copy-start.54
  80.0 7.7 copy-start.62
  80.9 6.8 copy-start.45
  88.5 49.3 %copy-start.1 = (bf16[2,192,768]{2,1,0:T(8,128)(2,1)S(1)}, bf16[2,192,768]{2,1,0:T(8,128)(2,1)}, u32[]{:S(2)}) copy-start(bf16[2,192,768]{2,1,0:T(8,128)(2,1)} %param.36) | copy-start | bytes 1769476
  90.8 101.1 %all-gather.9.cloned.1.call-start = ((), (), s32[]{:S(2)}) async-start(), calls=%async_computation.8 | async-start | bytes 2949120 | tf_op jit(solution)/shard_map/all_gather | solution.py:196
  91.5 50.5 %copy-start.13 = (bf16[2,3,768,192]{2,3,1,0:T(8,128)(2,1)S(1)}, bf16[2,3,768,192]{2,3,1,0:T(8,128)(2,1)}, u32[]{:S(2)}) copy-start(bf16[2,3,768,192]{2,3,1,0:T(8,128)(2,1)} %param.41) | copy-start | bytes 5308420
  137.8 2.8 copy-start.3
  141.7 126.0 %reduce-scatter.9.cloned.1.call-start = ((), (), s32[]{:S(2)}) async-start(), calls=%async_computation.9 | async-start | bytes 2949120 | tf_op jit(solution)/shard_map/reduce_scatter | solution.py:210
  143.1 52.2 %copy-start.53 = (bf16[1,1,768,192]{2,3,1,0:T(8,128)(2,1)S(1)}, bf16[1,1,768,192]{2,3,1,0:T(8,128)(2,1)}, u32[]{:S(2)}) copy-start(bf16[1,1,768,192]{2,3,1,0:T(8,128)(2,1)} %get-tuple-element.229) | copy-start | bytes 884740
  191.8 3.5 copy-start.94
  193.6 3.1 copy-start.58
  196.0 7.2 copy-start.49
  196.7 6.5 copy-start.47
  203.2 8.1 copy-start.64
  203.3 7.4 copy-start.51
  210.2 7.8 copy-start.66
  210.6 7.3 copy-start.56
  211.3 6.7 copy-start.28
  220.7 100.2 %all-gather.11.cloned.1.call-start = ((), (), s32[]{:S(2)}) async-start(), calls=%async_computation.10 | async-start | bytes 2949120 | tf_op jit(solution)/shard_map/all_gather | solution.py:196
  270.8 118.7 %reduce-scatter.11.cloned.1.call-start = ((), (), s32[]{:S(2)}) async-start(), calls=%async_computation.11 | async-start | bytes 2949120 | tf_op jit(solution)/shard_map/reduce_scatter | solution.py:210
  323.4 3.4 copy-start.16
  326.8 11.2 %copy-start.7 = (f32[2,512,768]{2,1,0:T(8,128)}, f32[2,512,768]{2,1,0:T(8,128)S(1)}, u32[]{:S(2)}) copy-start(f32[2,512,768]{2,1,0:T(8,128)S(1)} %fusion.46) | copy-start | bytes 9437188
  326.8 11.2 %copy-start.88 = (bf16[2,768,768]{2,1,0:T(8,128)(2,1)S(1)}, bf16[2,768,768]{2,1,0:T(8,128)(2,1)}, u32[]{:S(2)}) copy-start(bf16[2,768,768]{2,1,0:T(8,128)(2,1)} %param.44) | copy-start | bytes 7077892
  342.4 102.1 %all-gather.13.cloned.1.call-start = ((), (), s32[]{:S(2)}) async-start(), calls=%async_computation.12 | async-start | bytes 2949120 | tf_op jit(solution)/shard_map/all_gather | solution.py:196
  342.5 162.2 %copy-start.68 = (f32[192]{0:T(256)}, f32[192]{0:T(256)S(1)}, u32[]{:S(2)}) copy-start(f32[192]{0:T(256)S(1)} %get-tuple-element.250) | copy-start | bytes 2308
  394.4 110.3 %reduce-scatter.13.cloned.1.call-start = ((), (), s32[]{:S(2)}) async-start(), calls=%async_computation.13 | async-start | bytes 2949120 | tf_op jit(solution)/shard_map/reduce_scatter | solution.py:200
  447.0 3.0 copy-start.8
  447.0 3.0 copy-start.17
  450.0 3.8 copy-start.91
  457.7 103.9 %all-gather.15.cloned.1.call-start = ((), (), s32[]{:S(2)}) async-start(), calls=%async_computation.14 | async-start | bytes 2949120 | tf_op jit(solution)/shard_map/all_gather | solution.py:196
  504.7 5.5 copy-start.6
  510.2 3.2 copy-start.65
  510.2 3.2 copy-start.67
  510.2 64.9 %slice-start.4 = ((s8[14155776]{0:T(1024)(128)(4,1)}), s8[1572864]{0:T(1024)(128)(4,1)S(1)}, s32[]{:S(2)}) async-start(s8[14155776]{0:T(1024)(128)(4,1)} %bitcast.357), calls=%async_computation.23 | async-start | bytes 3145728
  511.4 132.8 %reduce-scatter.15.cloned.1.call-start = ((), (), s32[]{:S(2)}) async-start(), calls=%async_computation.15 | async-start | bytes 2949120 | tf_op jit(solution)/shard_map/reduce_scatter | solution.py:200
  563.2 12.0 %slice-start.5 = ((s8[14155776]{0:T(1024)(128)(4,1)}), s8[4194304]{0:T(1024)(128)(4,1)S(1)}, s32[]{:S(2)}) async-start(s8[14155776]{0:T(1024)(128)(4,1)} %bitcast.357), calls=%async_computation.24 | async-start | bytes 8388608
  565.5 7.5 copy-start.14
  565.5 9.7 %slice-start.6 = ((s8[14155776]{0:T(1024)(128)(4,1)}), s8[4194304]{0:T(1024)(128)(4,1)S(1)}, s32[]{:S(2)}) async-start(s8[14155776]{0:T(1024)(128)(4,1)} %bitcast.357), calls=%async_computation.25 | async-start | bytes 8388608
  565.5 9.7 %slice-start.7 = ((s8[14155776]{0:T(1024)(128)(4,1)}), s8[4194304]{0:T(1024)(128)(4,1)S(1)}, s32[]{:S(2)}) async-start(s8[14155776]{0:T(1024)(128)(4,1)} %bitcast.357), calls=%async_computation.26 | async-start | bytes 8388608
  581.8 6.9 copy-start.48
  581.8 6.9 copy-start.61
  591.0 2.8 copy-start.31
  597.2 47.0 %copy-start.2 = (bf16[2,192,768]{2,1,0:T(8,128)(2,1)S(1)}, bf16[2,192,768]{2,1,0:T(8,128)(2,1)}, u32[]{:S(2)}) copy-start(bf16[2,192,768]{2,1,0:T(8,128)(2,1)} %param.36) | copy-start | bytes 1769476
  597.2 47.0 %copy-start.4 = (bf16[2,192,768]{2,1,0:T(8,128)(2,1)S(1)}, bf16[2,192,768]{2,1,0:T(8,128)(2,1)}, u32[]{:S(2)}) copy-start(bf16[2,192,768]{2,1,0:T(8,128)(2,1)} %reduce-scatter.7.cloned.1.call-done) | copy-start | bytes 1769476
  597.2 47.0 %copy-start.69 = (f32[192]{0:T(256)S(1)}, f32[192]{0:T(256)}, u32[]{:S(2)}) copy-start(f32[192]{0:T(256)} %copy-done.68) | copy-start | bytes 2308
  597.2 102.5 %all-gather.17.cloned.1.call-start = ((), (), s32[]{:S(2)}) async-start(), calls=%async_computation.16 | async-start | bytes 2949120 | tf_op jit(solution)/shard_map/all_gather | solution.py:196
  649.5 213.2 %all-reduce.7.cloned.1.call-start = ((), (), s32[]{:S(2)}) async-start(), calls=%async_computation.18 | async-start | bytes 16515072 | tf_op jit(solution)/shard_map/psum | solution.py:319
  655.1 3.5 copy-start.96
  702.3 7.5 copy-start.46
  702.3 17.8 %slice-start = ((s8[14155776]{0:T(1024)(128)(4,1)}), s8[4194304]{0:T(1024)(128)(4,1)S(1)}, s32[]{:S(2)}) async-start(s8[14155776]{0:T(1024)(128)(4,1)} %bitcast.355), calls=%async_computation.19 | async-start | bytes 8388608
  702.3 17.8 %slice-start.1 = ((s8[14155776]{0:T(1024)(128)(4,1)}), s8[4194304]{0:T(1024)(128)(4,1)S(1)}, s32[]{:S(2)}) async-start(s8[14155776]{0:T(1024)(128)(4,1)} %bitcast.355), calls=%async_computation.20 | async-start | bytes 8388608
  709.8 10.3 %slice-start.2 = ((s8[14155776]{0:T(1024)(128)(4,1)}), s8[4194304]{0:T(1024)(128)(4,1)S(1)}, s32[]{:S(2)}) async-start(s8[14155776]{0:T(1024)(128)(4,1)} %bitcast.355), calls=%async_computation.21 | async-start | bytes 8388608
  709.8 10.3 %slice-start.3 = ((s8[14155776]{0:T(1024)(128)(4,1)}), s8[1572864]{0:T(1024)(128)(4,1)S(1)}, s32[]{:S(2)}) async-start(s8[14155776]{0:T(1024)(128)(4,1)} %bitcast.355), calls=%async_computation.22 | async-start | bytes 3145728
  720.1 7.0 copy-start.25
  735.8 177.8 %reduce-scatter.17.cloned.1.call-start = ((), (), s32[]{:S(2)}) async-start(), calls=%async_computation.17 | async-start | bytes 2949120 | tf_op jit(solution)/shard_map/reduce_scatter | solution.py:200
  862.7 4.1 copy-start.36
  871.3 2.9 copy-start.26
  874.1 39.5 %copy-start.10 = (f32[2,192,768]{2,1,0:T(8,128)S(1)}, f32[2,192,768]{2,1,0:T(8,128)}, u32[]{:S(2)}) copy-start(f32[2,192,768]{2,1,0:T(8,128)} %copy-done.9) | copy-start | bytes 3538948
  (56 other events, 84.6 us)
Sparse Core Ops, SparseCore 0:
  9.6 53.1 all-gather.6
  90.9 46.8 reduce-scatter.6
  141.8 49.9 all-gather.8
  220.8 46.8 reduce-scatter.8
  270.9 49.9 all-gather.10
  342.5 46.8 reduce-scatter.10
  394.5 49.9 all-gather.12
  457.8 46.8 reduce-scatter.12
  511.6 49.9 all-gather.14
  597.3 46.8 reduce-scatter.14
  649.7 49.9 all-gather.16
  735.9 126.7 all-reduce.6
  865.1 48.4 reduce-scatter.16
